TPU v7x, 256 devices: a whole 4x4x8 slice. The times are simulated.
256 devices in a mesh: seq: 32 (over y_lo, z, core), tp: 8 (over x, y_hi).
Axes of the slice: x: 4, y: 4 (y_hi: 2, y_lo: 2; y = y_hi * 2 + y_lo), z: 8, core: 2. Of those that a mesh axis runs over, the one named last changes fastest.
Arguments:
- query: bfloat16 [6144, 5120], P('seq', 'tp')
- span_keys: bfloat16 [6144, 5120], P('seq', 'tp'), may hold values from -6 to 6
- span_values: bfloat16 [6144, 5120], P('seq', 'tp'), may hold values from -48 to 48
- cache_keys: bfloat16 [8, 8192, 5120], P(None, 'seq', 'tp'), may hold values from -6 to 6
- cache_values: bfloat16 [8, 8192, 5120], P(None, 'seq', 'tp'), may hold values from -48 to 48
- out_weight: bfloat16 [5120, 5120], P('tp'), may hold values from -0.078125 to 0.078125
- cache_lengths: int32 [8], replicated, may hold values from 1 to 8192, as said below
- sink_counts: int32 [8], replicated, may hold values from 1 to 256, as said below
- windows: int32 [8], replicated, may hold values from 2048 to 4096, as said below
- block_of_slot: int32 [8, 32], replicated, may hold values from 0 to 31, each once within a row
Outputs:
- projected: bfloat16 [6144, 5120], P('seq', 'tp')
Inputs may be any that keep to these rules, and one draw needn't show every extreme that they name: `cache_lengths`: at least 1 and at most 8192; some request has exactly 8192. `sink_counts`: some request has exactly 256. `windows`: some request has exactly 4096. `block_of_slot`: each row is a permutation of 0 to 31.
All inputs are finite; a program needn't handle non-finite values.
Results may differ from a plain program's by a relative error of at most 0.015.
Values may be sent and summed in bfloat16 or wider, within the bound.
A program may use at most 192 MiB of HBM per device.

v0:
```python
import math
import jax
import jax.numpy as jnp
import numpy as np
from jax import lax
from jax.sharding import Mesh
from jax.sharding import PartitionSpec as P

HEAD = 128
GROUP = 4
NEG = -1e30


def visible(query_pos, key_pos, valid, window, sinks):
    later = query_pos[:, None]
    earlier = key_pos[None, :]
    near = later - earlier < window
    return (earlier <= later) & (near | (earlier < sinks)) & valid[None, :]


def block_partial(q_rows, keys, vals, query_pos, key_pos, valid, window, sinks):
    mask = visible(query_pos, key_pos, valid, window, sinks)
    scale = 1.0 / math.sqrt(q_rows.shape[-1])
    scores = jnp.einsum("qhd,khd->hqk", q_rows, keys, preferred_element_type=jnp.float32) * scale
    scores = jnp.where(mask[None], scores, NEG)
    top = jnp.max(scores, axis=2)
    weights = jnp.where(mask[None], jnp.exp(scores - top[:, :, None]), 0.0)
    total = jnp.sum(weights, axis=2)
    summed = jnp.einsum(
        "hqk,khd->qhd", weights.astype(jnp.bfloat16), vals, preferred_element_type=jnp.float32
    )
    return (summed, top.T, total.T)


def shards(
    query,
    span_keys,
    span_values,
    cache_keys,
    cache_values,
    out_weight,
    cache_lengths,
    sink_counts,
    windows,
    block_of_slot,
):
    rows, width = query.shape
    heads_here = width // HEAD
    places = lax.axis_size("place")
    group = lax.axis_size("req")
    place = lax.axis_index("place")
    mine = lax.axis_index("req")
    cache_dev = cache_keys.shape[1]
    length = cache_lengths[mine]
    window = windows[mine]
    sinks = sink_counts[mine]
    got_keys = lax.all_to_all(cache_keys, "req", split_axis=0, concat_axis=0, tiled=True)
    got_vals = lax.all_to_all(cache_values, "req", split_axis=0, concat_axis=0, tiled=True)
    span_q = lax.all_gather(query, "place", axis=0, tiled=True)
    blocks = lax.dynamic_slice_in_dim(block_of_slot[mine], place * group, group)
    slot_pos = (
        blocks[:, None] * cache_dev + jnp.arange(cache_dev, dtype=jnp.int32)[None, :]
    ).reshape(-1)
    own_pos = length + place * rows + jnp.arange(rows, dtype=jnp.int32)
    query_pos = length + jnp.arange(places * rows, dtype=jnp.int32)
    keys = jnp.concatenate([got_keys.reshape(-1, width), span_keys], 0).reshape(
        -1, heads_here, HEAD
    )
    vals = jnp.concatenate([got_vals.reshape(-1, width), span_values], 0).reshape(
        -1, heads_here, HEAD
    )
    key_pos = jnp.concatenate([slot_pos, own_pos])
    valid = jnp.concatenate([slot_pos < length, jnp.ones((rows,), jnp.bool_)])
    summed, top, total = block_partial(
        span_q.reshape(-1, heads_here, HEAD), keys, vals, query_pos, key_pos, valid, window, sinks
    )
    summed = lax.all_to_all(
        summed.reshape(places, rows, width), "place", split_axis=0, concat_axis=0, tiled=True
    ).reshape(places, rows, heads_here, HEAD)
    stats = jnp.concatenate([top, total], axis=1).reshape(places, rows, 2 * heads_here)
    stats = lax.all_to_all(stats, "place", split_axis=0, concat_axis=0, tiled=True)
    top, total = (stats[..., :heads_here], stats[..., heads_here:])
    best = jnp.max(top, axis=0)
    factor = jnp.exp(top - best[None])
    total = jnp.sum(total * factor, axis=0)
    summed = jnp.sum(summed * factor[..., None], axis=0)
    attention = (summed / total[..., None]).astype(jnp.bfloat16).reshape(rows, width)
    terms = jnp.dot(attention, out_weight, preferred_element_type=jnp.float32)
    return lax.psum_scatter(terms.astype(jnp.bfloat16), "tp", scatter_dimension=1, tiled=True)


def solution(mesh):
    seq_size = mesh.shape["seq"]
    requests = 8
    grid = Mesh(
        np.asarray(mesh.devices).reshape(seq_size // requests, requests, mesh.shape["tp"]),
        ("place", "req", "tp"),
    )
    seq = ("place", "req")
    return jax.shard_map(
        shards,
        mesh=grid,
        in_specs=(
            P(seq, "tp"),
            P(seq, "tp"),
            P(seq, "tp"),
            P(None, seq, "tp"),
            P(None, seq, "tp"),
            P("tp", None),
            P(),
            P(),
            P(),
            P(),
        ),
        out_specs=P(seq, "tp"),
        check_vma=False,
    )
```

profile of v0, /device:TPU:2, one launch (start us, length us, event | category | flops | bytes accessed | tf_op | source)
XLA Modules:
  0.0 391.5 jit_solution(4118115496891298422)
XLA Ops:
  6.5 66.3 %all_to_all.20 = bf16[8,256,640]{2,1,0:T(8,128)(2,1)} all-to-all(bf16[8,256,640]{2,1,0:T(8,128)(2,1)} %param.14), channel_id=1, replica_groups=mesh['place'=4,'req'=8,'tp'=8] {'req'}, dimensions={0} | all-to-all | bytes 5242880 | tf_op jit(solution)/shard_map/all_to_all | solution.py:58
  72.8 0.0 copy-start.2
  72.8 3.8 all-to-all-start.1
  76.6 0.7 dynamic_slice.15
  77.3 0.6 dynamic_slice.16
  77.9 0.7 dynamic_slice.14
  78.5 0.8 multiply_bitcast_fusion
  79.3 0.1 add_bitcast_fusion
  79.4 0.2 copy.38
  79.6 0.9 copy.40
  80.4 1.1 copy.34
  81.6 0.2 copy.36
  81.8 77.9 %all_gather.3 = bf16[768,640]{1,0:T(8,128)(2,1)} all-gather(bf16[192,640]{1,0:T(8,128)(2,1)S(1)} %copy-done.2), channel_id=1, replica_groups=mesh['place'=4,'req'=8,'tp'=8] {'place'}, dimensions={0}, use_global_device_ids=true | all-gather | bytes 1228800 | tf_op jit(solution)/shard_map/all_gather | solution.py:59
  159.7 2.3 copy.41
  162.6 0.7 broadcast_compare_fusion.1
  163.3 0.6 broadcast_compare_fusion
  163.9 0.7 iota_add_fusion
  164.6 4.6 %fusion.7 = pred[768,2240]{0,1:T(8,128)(4,1)} fusion(s32[]{:T(128)} %bitcast.3, s32[768]{0:T(1024)S(1)} %iota_add_fusion, s32[2240]{0:T(1024)S(1)} %pad_add_fusion, pred[2240]{0:T(1024)(128)(4,1)S(1)} %concatenate.33, pred[2240]{0:T(1024)(128)(4,1)S(1)} %broadcast_compare_fusion), kind=kLoop, calls=%fused_computation.9 | loop fusion | flops 10321920 | bytes 1736836 | tf_op jit(solution)/shard_map/and | solution.py:18
  169.2 7.0 %reshape.156 = bf16[2048,5,128]{2,1,0:T(8,128)(2,1)} reshape(bf16[8,256,640]{2,1,0:T(8,128)(2,1)} %all_to_all.20) | data formatting | bytes 5242880 | tf_op jit(solution)/shard_map/concatenate | solution.py:69
  176.2 4.0 %copy.35 = bf16[2048,5,128]{2,0,1:T(8,128)(2,1)} copy(bf16[2048,5,128]{2,1,0:T(8,128)(2,1)} %reshape.156) | data formatting | bytes 5242880 | tf_op jit(solution)/shard_map/concatenate | solution.py:69
  180.3 0.0 all-to-all-done.1
  180.3 4.2 %reshape.157 = bf16[2048,5,128]{2,1,0:T(8,128)(2,1)} reshape(bf16[8,256,640]{2,1,0:T(8,128)(2,1)S(1)} %all-to-all-done.1) | data formatting | bytes 5242880 | tf_op jit(solution)/shard_map/concatenate | solution.py:66
  184.5 2.7 copy.39
  187.2 0.0 copy-done
  187.2 0.3 copy-done.1
  187.4 0.0 copy-done.4
  187.5 13.8 %fusion.25 = (f32[5,768]{1,0:T(8,128)S(1)}, f32[5,768,2240]{1,2,0:T(8,128)}) fusion(bf16[768,5,128]{0,2,1:T(8,128)(2,1)S(1)} %bitcast.41, bf16[192,5,128]{2,0,1:T(8,128)(2,1)S(1)} %copy-done.4, bf16[2048,5,128]{2,0,1:T(8,128)(2,1)S(1)} %copy.39, pred[768,2240]{0,1:T(8,128)(4,1)S(1)} %copy-done), kind=kOutput, calls=%fused_computation.37 | convolution fusion | flops 2233544960 | bytes 39992320 | tf_op jit(solution)/shard_map/qhd,khd->hqk/dot_general | solution.py:24
  201.3 14.2 %fusion = f32[5,768]{1,0:T(8,128)S(1)} fusion(f32[5,768,2240]{1,2,0:T(8,128)} %get-tuple-element.8, f32[5,768]{1,0:T(8,128)S(1)} %get-tuple-element.7, pred[768,2240]{0,1:T(8,128)(4,1)S(1)} %copy-done), kind=kLoop, calls=%fused_computation.2 | loop fusion | flops 25800960 | bytes 36157440 | tf_op jit(solution)/shard_map/reduce_sum | solution.py:28
  215.5 0.1 reshape.155
  215.6 0.7 reshape.160
  216.3 3.8 all-to-all-start.3
  220.1 16.6 %fusion.15 = f32[768,5,128]{0,2,1:T(8,128)} fusion(f32[5,768,2240]{1,2,0:T(8,128)} %get-tuple-element.8, f32[5,768]{1,0:T(8,128)S(1)} %get-tuple-element.7, pred[768,2240]{0,1:T(8,128)(4,1)S(1)} %copy-done, bf16[192,5,128]{2,0,1:T(8,128)(2,1)S(1)} %copy.36, bf16[2048,5,128]{2,0,1:T(8,128)(2,1)} %copy.35), kind=kOutput, calls=%fused_computation.19 | convolution fusion | flops 2233548800 | bytes 40975360 | tf_op jit(solution)/shard_map/hqk,khd->qhd/dot_general | solution.py:29
  236.7 3.1 reshape.154
  239.8 2.5 copy.43
  242.4 0.0 all-to-all-done.3
  242.4 8.1 %all-to-all-start.2 = ((f32[4,192,640]{2,1,0:T(8,128)}), f32[4,192,640]{2,1,0:T(8,128)}, u32[]{:S(2)}, u32[]{:S(2)}) async-start(f32[4,192,640]{2,1,0:T(8,128)} %copy.43), calls=%async_computation.2 | async-start | bytes 3932160 | tf_op jit(solution)/shard_map/all_to_all | solution.py:77
  250.5 0.5 broadcast.100
  251.0 0.7 reduce.1
  251.7 0.1 reshape.161
  251.8 35.7 %all-to-all-done.2 = f32[4,192,640]{2,1,0:T(8,128)} async-done(((f32[4,192,640]{2,1,0:T(8,128)}), f32[4,192,640]{2,1,0:T(8,128)}, u32[]{:S(2)}, u32[]{:S(2)}) %all-to-all-start.2) | async-done | bytes 1966112 | tf_op jit(solution)/shard_map/all_to_all | solution.py:77
  287.5 2.0 copy.45
  289.6 0.2 fusion.14
  289.8 0.1 fusion.20
  289.9 4.6 %convolution_convert_fusion = bf16[192,5120]{1,0:T(8,128)(2,1)S(1)} fusion(bf16[192,640]{0,1:T(8,128)(2,1)S(1)} %fusion.20, bf16[640,5120]{1,0:T(8,128)(2,1)} %param.15), kind=kOutput, calls=%fused_computation.10 | convolution fusion | flops 1259274240 | bytes 8765440 | tf_op jit(solution)/shard_map/dot_general | solution.py:88
  294.5 2.6 copy.51
  297.0 0.0 reduce-scatter.4.cloned.1.call-update
  297.1 85.7 %reduce-scatter.4.cloned.1.call-done = bf16[640,192]{1,0:T(8,128)(2,1)} async-done(((bf16[5120,192]{1,0:T(8,128)(2,1)}), bf16[640,192]{1,0:T(8,128)(2,1)}) %reduce-scatter.4.cloned.1.call-update) | async-done | bytes 245776
  382.8 1.8 copy.52
  (21 shorter events, 0.1 us)
Async XLA Ops:
  72.8 3.8 copy-start.5
  72.8 4.5 %copy-start.6 = (s32[8]{0:T(128)S(1)}, s32[8]{0:T(128)}, u32[]{:S(2)}) copy-start(s32[8]{0:T(128)} %param.17) | copy-start | bytes 100
  72.8 5.1 %copy-start.7 = (s32[8]{0:T(128)S(1)}, s32[8]{0:T(128)}, u32[]{:S(2)}) copy-start(s32[8]{0:T(128)} %param.16) | copy-start | bytes 100
  72.8 6.6 %copy-start.3 = (bf16[192,640]{1,0:T(8,128)(2,1)S(1)}, bf16[192,640]{1,0:T(8,128)(2,1)}, u32[]{:S(2)}) copy-start(bf16[192,640]{1,0:T(8,128)(2,1)} %param.11) | copy-start | bytes 737284
  72.8 8.9 %copy-start.2 = (bf16[192,640]{1,0:T(8,128)(2,1)S(1)}, bf16[192,640]{1,0:T(8,128)(2,1)}, u32[]{:S(2)}) copy-start(bf16[192,640]{1,0:T(8,128)(2,1)} %param.10) | copy-start | bytes 737284
  72.8 107.4 %all-to-all-start.1 = ((bf16[8,256,640]{2,1,0:T(8,128)(2,1)}), bf16[8,256,640]{2,1,0:T(8,128)(2,1)S(1)}, u32[]{:S(2)}, u32[]{:S(2)}) async-start(bf16[8,256,640]{2,1,0:T(8,128)(2,1)} %param.13), calls=%async_computation.1 | async-start | bytes 5242880 | tf_op jit(solution)/shard_map/all_to_all | solution.py:57
  184.5 2.7 copy-start
  184.5 3.0 copy-start.1
  184.5 3.0 copy-start.4
  216.3 26.1 %all-to-all-start.3 = ((f32[4,1,1920]{2,1,0:T(1,128)}), f32[4,1,1920]{2,1,0:T(1,128)S(1)}, u32[]{:S(2)}, u32[]{:S(2)}) async-start(f32[4,1,1920]{2,1,0:T(1,128)} %reshape.160), calls=%async_computation.3 | async-start | bytes 61440 | tf_op jit(solution)/shard_map/all_to_all | solution.py:81
  242.4 45.2 %all-to-all-start.2 = ((f32[4,192,640]{2,1,0:T(8,128)}), f32[4,192,640]{2,1,0:T(8,128)}, u32[]{:S(2)}, u32[]{:S(2)}) async-start(f32[4,192,640]{2,1,0:T(8,128)} %copy.43), calls=%async_computation.2 | async-start | bytes 3932160 | tf_op jit(solution)/shard_map/all_to_all | solution.py:77
  250.5 132.3 %reduce-scatter.4.cloned.1.call-start = ((), (), s32[]{:S(2)}) async-start(), calls=%async_computation.5 | async-start | bytes 2949120
Sparse Core Ops, SparseCore 0:
  297.2 85.5 reduce-scatter.3
where the time goes:
time: 392 us; the launch traced here: 391 us
  blocking collectives  144 us (37%)
  waiting for transfers between devices  121 us (31%)
  local copies, waits for them, and re-layouts  38.3 us (10%)
  matrix products  35 us (9%)
  other arithmetic  22.6 us (6%)
  starting transfers between devices  15.7 us (4%)
  between operations  14.3 us (4%)
    unnamed x2, waiting for transfers between devices  85.7 us
    all_gather x1, blocking collectives, shards(): span_q = lax.all_gather(query, 'place', axis=0, tiled=True)  77.9 us
    all_to_all x1, blocking collectives, shards(): lax.all_to_all(cache_values, 'req', split_axis=0, concat_axis=0, tiled=True)  66.3 us
    all_to_all x1, waiting for transfers between devices, shards(): lax.all_to_all(summed.reshape(places, rows, width), 'place', split_axis=0...  35.7 us
    dot_general x1, matrix products, block_partial(): jnp.einsum('hqk,khd->qhd', weights.astype(jnp.bfloat16), vals, preferred_...  16.6 us
    reduce_sum x1, other arithmetic, block_partial(): total = jnp.sum(weights, axis=2)  14.2 us
    dot_general x1, matrix products, block_partial(): jnp.einsum('qhd,khd->hqk', q_rows, keys, preferred_element_type=jnp.float32)  13.8 us
    concatenate x3, local copies, waits for them, and re-layouts, shards(): jnp.concatenate([got_vals.reshape(-1, width), span_values], 0)  11.2 us
  transfers between devices with their start and end apart: 4, of which 2 were waited for; matrix products, arithmetic and copies ran while one was open for 12% of the time, Pallas kernels for 0%

commit v1 on v0

--- a/solution.py
+++ b/solution.py
@@ -9,6 +9,13 @@
 HEAD = 128
 GROUP = 4
 NEG = -1e30
+
+
+def store_core(target):
+    reached = jnp.concatenate(
+        lax.all_to_all(jnp.stack([target] * lax.axis_size("place")), "place", 0, 0), axis=0
+    )
+    return reached
 
 
 def visible(query_pos, key_pos, valid, window, sinks):
@@ -56,7 +63,7 @@
     sinks = sink_counts[mine]
     got_keys = lax.all_to_all(cache_keys, "req", split_axis=0, concat_axis=0, tiled=True)
     got_vals = lax.all_to_all(cache_values, "req", split_axis=0, concat_axis=0, tiled=True)
-    span_q = lax.all_gather(query, "place", axis=0, tiled=True)
+    span_q = store_core(query)
     blocks = lax.dynamic_slice_in_dim(block_of_slot[mine], place * group, group)
     slot_pos = (
         blocks[:, None] * cache_dev + jnp.arange(cache_dev, dtype=jnp.int32)[None, :]

time: 392 us -> 365 us (0.931)
  blocking collectives: 144 us -> 35.7 us
  waiting for transfers between devices: 121 us -> 196 us
  starting transfers between devices: 15.7 us -> 20.4 us
    all_gather x1 -> x0, blocking collectives: 77.9 us -> none  [shards(): span_q = lax.all_gather(query, 'place', axis=0, tiled=True)]
    all_to_all x1, waiting for transfers between devices: 0.01 us -> 53.4 us  [shards(): lax.all_to_all(cache_keys, 'req', split_axis=0, concat_axis=0, tiled=True)]
    all_to_all x1, blocking collectives: 66.3 us -> 35.7 us  [store_core(): lax.all_to_all(jnp.stack([target] * lax.axis_size('place')), 'place', 0, 0)]
    all_to_all x0 -> x1, waiting for transfers between devices: none -> 15.5 us  [shards(): lax.all_to_all(cache_values, 'req', split_axis=0, concat_axis=0, tiled=True)]
    all_to_all x1, waiting for transfers between devices: 35.7 us -> 44.1 us  [shards(): lax.all_to_all(summed.reshape(places, rows, width), 'place', split_axis=0...]
    another operation x0 -> x2, local copies, waits for them, and re-layouts: none -> 4.52 us  [the longest x1 3.5 us: shards(): span_q.reshape(-1, heads_here, HEAD)]
    all_to_all x0 -> x1, starting transfers between devices: none -> 4.42 us  [shards(): lax.all_to_all(cache_values, 'req', split_axis=0, concat_axis=0, tiled=True)]
  transfers between devices with their start and end apart: 4 -> 5, of which waited for: 2 -> 4; matrix products, arithmetic and copies ran while one was open for 12% -> 23% of each run, Pallas kernels for 0% -> 0%
where the time goes in v1:
time: 365 us; the launch traced here: 364 us
  waiting for transfers between devices  196 us (54%)
  local copies, waits for them, and re-layouts  39.8 us (11%)
  blocking collectives  35.7 us (10%)
  matrix products  35.4 us (10%)
  other arithmetic  22.7 us (6%)
  starting transfers between devices  20.4 us (6%)
  between operations  14.3 us (4%)
    unnamed x2, waiting for transfers between devices  83.3 us
    all_to_all x1, waiting for transfers between devices, shards(): lax.all_to_all(cache_keys, 'req', split_axis=0, concat_axis=0, tiled=True)  53.4 us
    all_to_all x1, waiting for transfers between devices, shards(): lax.all_to_all(summed.reshape(places, rows, width), 'place', split_axis=0...  44.1 us
    all_to_all x1, blocking collectives, store_core(): lax.all_to_all(jnp.stack([target] * lax.axis_size('place')), 'place', 0, 0)  35.7 us
    dot_general x1, matrix products, block_partial(): jnp.einsum('hqk,khd->qhd', weights.astype(jnp.bfloat16), vals, preferred_...  16.6 us
    all_to_all x1, waiting for transfers between devices, shards(): lax.all_to_all(cache_values, 'req', split_axis=0, concat_axis=0, tiled=True)  15.5 us
    dot_general x1, matrix products, block_partial(): jnp.einsum('qhd,khd->hqk', q_rows, keys, preferred_element_type=jnp.float32)  14.3 us
    reduce_sum x1, other arithmetic, block_partial(): total = jnp.sum(weights, axis=2)  14.2 us
  transfers between devices with their start and end apart: 5, of which 4 were waited for; matrix products, arithmetic and copies ran while one was open for 23% of the time, Pallas kernels for 0%

profile of v1, /device:TPU:2, one launch (start us, length us, event | category | flops | bytes accessed | tf_op | source)
XLA Modules:
  0.0 364.4 jit_solution(187640124922260332)
XLA Ops:
  6.5 1.0 stack.2
  7.6 35.7 %all_to_all.25 = bf16[4,192,640]{2,1,0:T(8,128)(2,1)} all-to-all(bf16[4,192,640]{2,1,0:T(8,128)(2,1)S(1)} %stack.2), channel_id=1, replica_groups=mesh['place'=4,'req'=8,'tp'=8] {'place'}, dimensions={0} | all-to-all | bytes 1966080 | tf_op jit(solution)/shard_map/all_to_all | solution.py:16
  43.2 4.7 %all-to-all-start.1 = ((bf16[8,256,640]{2,1,0:T(8,128)(2,1)}), bf16[8,256,640]{2,1,0:T(8,128)(2,1)S(1)}, u32[]{:S(2)}, u32[]{:S(2)}) async-start(bf16[8,256,640]{2,1,0:T(8,128)(2,1)} %param.13), calls=%async_computation.1 | async-start | bytes 5242880 | tf_op jit(solution)/shard_map/all_to_all | solution.py:64
  47.9 0.8 multiply_bitcast_fusion
  48.7 0.1 add_bitcast_fusion
  48.8 0.7 dynamic_slice.14
  49.4 0.6 dynamic_slice.16
  50.0 0.7 dynamic_slice.15
  50.7 0.2 copy.38
  50.8 0.9 copy.40
  51.7 0.2 copy.34
  51.9 0.2 copy.36
  52.8 0.7 broadcast_compare_fusion.1
  53.5 0.6 broadcast_compare_fusion
  54.1 0.7 iota_add_fusion
  54.8 53.4 %all-to-all-done.1 = bf16[8,256,640]{2,1,0:T(8,128)(2,1)S(1)} async-done(((bf16[8,256,640]{2,1,0:T(8,128)(2,1)}), bf16[8,256,640]{2,1,0:T(8,128)(2,1)S(1)}, u32[]{:S(2)}, u32[]{:S(2)}) %all-to-all-start.1) | async-done | bytes 2621472 | tf_op jit(solution)/shard_map/all_to_all | solution.py:64
  108.2 4.4 %all-to-all-start = ((bf16[8,256,640]{2,1,0:T(8,128)(2,1)}), bf16[8,256,640]{2,1,0:T(8,128)(2,1)}, u32[]{:S(2)}, u32[]{:S(2)}) async-start(bf16[8,256,640]{2,1,0:T(8,128)(2,1)} %param.14), calls=%async_computation | async-start | bytes 5242880 | tf_op jit(solution)/shard_map/all_to_all | solution.py:65
  112.6 4.6 %fusion.7 = pred[768,2240]{0,1:T(8,128)(4,1)} fusion(s32[]{:T(128)} %bitcast.3, s32[768]{0:T(1024)S(1)} %iota_add_fusion, s32[2240]{0:T(1024)S(1)} %pad_add_fusion, pred[2240]{0:T(1024)(128)(4,1)S(1)} %concatenate.33, pred[2240]{0:T(1024)(128)(4,1)S(1)} %broadcast_compare_fusion), kind=kLoop, calls=%fused_computation.9 | loop fusion | flops 10321920 | bytes 1736836 | tf_op jit(solution)/shard_map/and | solution.py:25
  117.2 3.5 reshape.156
  120.7 4.2 %reshape.155 = bf16[2048,5,128]{2,1,0:T(8,128)(2,1)} reshape(bf16[8,256,640]{2,1,0:T(8,128)(2,1)S(1)} %all-to-all-done.1) | data formatting | bytes 5242880 | tf_op jit(solution)/shard_map/concatenate | solution.py:73
  124.9 2.7 copy.39
  127.6 0.0 copy-done
  127.6 0.5 copy-done.1
  128.1 0.0 copy-done.4
  128.1 14.3 %fusion.26 = (f32[5,768]{1,0:T(8,128)S(1)}, f32[5,768,2240]{1,2,0:T(8,128)}) fusion(bf16[768,5,128]{2,1,0:T(8,128)(2,1)S(1)} %copy-done.1, bf16[192,5,128]{2,0,1:T(8,128)(2,1)S(1)} %copy-done.4, bf16[2048,5,128]{2,0,1:T(8,128)(2,1)S(1)} %copy.39, pred[768,2240]{0,1:T(8,128)(4,1)S(1)} %copy-done), kind=kOutput, calls=%fused_computation.38 | convolution fusion | flops 2233544960 | bytes 39992320 | tf_op jit(solution)/shard_map/qhd,khd->hqk/dot_general | solution.py:31
  142.4 14.2 %fusion = f32[5,768]{1,0:T(8,128)S(1)} fusion(f32[5,768,2240]{1,2,0:T(8,128)} %get-tuple-element.8, f32[5,768]{1,0:T(8,128)S(1)} %get-tuple-element.7, pred[768,2240]{0,1:T(8,128)(4,1)S(1)} %copy-done), kind=kLoop, calls=%fused_computation.2 | loop fusion | flops 25800960 | bytes 36157440 | tf_op jit(solution)/shard_map/reduce_sum | solution.py:35
  156.6 0.1 reshape.153
  156.7 0.7 reshape.159
  157.4 15.5 %all-to-all-done = bf16[8,256,640]{2,1,0:T(8,128)(2,1)} async-done(((bf16[8,256,640]{2,1,0:T(8,128)(2,1)}), bf16[8,256,640]{2,1,0:T(8,128)(2,1)}, u32[]{:S(2)}, u32[]{:S(2)}) %all-to-all-start) | async-done | bytes 2621472 | tf_op jit(solution)/shard_map/all_to_all | solution.py:65
  172.9 3.4 all-to-all-start.4
  176.3 7.0 %reshape.154 = bf16[2048,5,128]{2,1,0:T(8,128)(2,1)} reshape(bf16[8,256,640]{2,1,0:T(8,128)(2,1)} %all-to-all-done) | data formatting | bytes 5242880 | tf_op jit(solution)/shard_map/concatenate | solution.py:76
  183.3 4.0 %copy.35 = bf16[2048,5,128]{2,0,1:T(8,128)(2,1)} copy(bf16[2048,5,128]{2,1,0:T(8,128)(2,1)} %reshape.154) | data formatting | bytes 5242880 | tf_op jit(solution)/shard_map/concatenate | solution.py:76
  187.4 16.6 %fusion.15 = f32[768,5,128]{0,2,1:T(8,128)} fusion(f32[5,768,2240]{1,2,0:T(8,128)} %get-tuple-element.8, f32[5,768]{1,0:T(8,128)S(1)} %copy-done.6, pred[768,2240]{0,1:T(8,128)(4,1)S(1)} %copy-done, bf16[192,5,128]{2,0,1:T(8,128)(2,1)S(1)} %copy.36, bf16[2048,5,128]{2,0,1:T(8,128)(2,1)} %copy.35), kind=kOutput, calls=%fused_computation.19 | convolution fusion | flops 2233548800 | bytes 40975360 | tf_op jit(solution)/shard_map/hqk,khd->qhd/dot_general | solution.py:36
  203.9 3.1 reshape.152
  207.1 2.6 copy.43
  209.6 7.9 %all-to-all-start.3 = ((f32[4,192,640]{2,1,0:T(8,128)}), f32[4,192,640]{2,1,0:T(8,128)}, u32[]{:S(2)}, u32[]{:S(2)}) async-start(f32[4,192,640]{2,1,0:T(8,128)} %copy.43), calls=%async_computation.3 | async-start | bytes 3932160 | tf_op jit(solution)/shard_map/all_to_all | solution.py:84
  217.5 0.5 broadcast.102
  218.0 0.7 reduce.1
  218.7 0.1 reshape.160
  218.9 44.1 %all-to-all-done.3 = f32[4,192,640]{2,1,0:T(8,128)} async-done(((f32[4,192,640]{2,1,0:T(8,128)}), f32[4,192,640]{2,1,0:T(8,128)}, u32[]{:S(2)}, u32[]{:S(2)}) %all-to-all-start.3) | async-done | bytes 1966112 | tf_op jit(solution)/shard_map/all_to_all | solution.py:84
  262.9 2.0 copy.45
  265.0 0.2 fusion.14
  265.2 0.1 fusion.21
  265.3 4.6 %convolution_convert_fusion = bf16[192,5120]{1,0:T(8,128)(2,1)S(1)} fusion(bf16[192,640]{0,1:T(8,128)(2,1)S(1)} %fusion.21, bf16[640,5120]{1,0:T(8,128)(2,1)} %param.15), kind=kOutput, calls=%fused_computation.10 | convolution fusion | flops 1259274240 | bytes 8765440 | tf_op jit(solution)/shard_map/dot_general | solution.py:95
  269.9 2.5 copy.54
  272.4 0.0 reduce-scatter.4.cloned.1.call-update
  272.4 83.3 %reduce-scatter.4.cloned.1.call-done = bf16[640,192]{1,0:T(8,128)(2,1)} async-done(((bf16[5120,192]{1,0:T(8,128)(2,1)}), bf16[640,192]{1,0:T(8,128)(2,1)}) %reduce-scatter.4.cloned.1.call-update) | async-done | bytes 245776
  355.7 1.8 copy.55
  (27 shorter events, 0.1 us)
Async XLA Ops:
  43.2 5.5 %copy-start.7 = (s32[8]{0:T(128)S(1)}, s32[8]{0:T(128)}, u32[]{:S(2)}) copy-start(s32[8]{0:T(128)} %param.16) | copy-start | bytes 100
  43.2 6.2 %copy-start.8 = (s32[8]{0:T(128)S(1)}, s32[8]{0:T(128)}, u32[]{:S(2)}) copy-start(s32[8]{0:T(128)} %param.17) | copy-start | bytes 100
  43.2 6.8 %copy-start.9 = (s32[8]{0:T(128)S(1)}, s32[8]{0:T(128)}, u32[]{:S(2)}) copy-start(s32[8]{0:T(128)} %param.18) | copy-start | bytes 100
  43.2 7.4 %copy-start.2 = (bf16[192,640]{1,0:T(8,128)(2,1)S(1)}, bf16[192,640]{1,0:T(8,128)(2,1)}, u32[]{:S(2)}) copy-start(bf16[192,640]{1,0:T(8,128)(2,1)} %param.11) | copy-start | bytes 737284
  43.2 8.5 %copy-start.3 = (bf16[192,640]{1,0:T(8,128)(2,1)S(1)}, bf16[192,640]{1,0:T(8,128)(2,1)}, u32[]{:S(2)}) copy-start(bf16[192,640]{1,0:T(8,128)(2,1)} %param.12) | copy-start | bytes 737284
  43.2 64.9 %all-to-all-start.1 = ((bf16[8,256,640]{2,1,0:T(8,128)(2,1)}), bf16[8,256,640]{2,1,0:T(8,128)(2,1)S(1)}, u32[]{:S(2)}, u32[]{:S(2)}) async-start(bf16[8,256,640]{2,1,0:T(8,128)(2,1)} %param.13), calls=%async_computation.1 | async-start | bytes 5242880 | tf_op jit(solution)/shard_map/all_to_all | solution.py:64
  108.2 64.7 %all-to-all-start = ((bf16[8,256,640]{2,1,0:T(8,128)(2,1)}), bf16[8,256,640]{2,1,0:T(8,128)(2,1)}, u32[]{:S(2)}, u32[]{:S(2)}) async-start(bf16[8,256,640]{2,1,0:T(8,128)(2,1)} %param.14), calls=%async_computation | async-start | bytes 5242880 | tf_op jit(solution)/shard_map/all_to_all | solution.py:65
  124.9 2.7 copy-start
  124.9 3.2 copy-start.1
  124.9 3.2 copy-start.4
  142.4 14.2 %copy-start.5 = (f32[5,768]{1,0:T(8,128)}, f32[5,768]{1,0:T(8,128)S(1)}, u32[]{:S(2)}) copy-start(f32[5,768]{1,0:T(8,128)S(1)} %get-tuple-element.7) | copy-start | bytes 46084
  172.9 36.7 %all-to-all-start.4 = ((f32[4,1,1920]{2,1,0:T(1,128)}), f32[4,1,1920]{2,1,0:T(1,128)S(1)}, u32[]{:S(2)}, u32[]{:S(2)}) async-start(f32[4,1,1920]{2,1,0:T(1,128)} %reshape.159), calls=%async_computation.4 | async-start | bytes 61440 | tf_op jit(solution)/shard_map/all_to_all | solution.py:88
  183.3 4.0 %copy-start.6 = (f32[5,768]{1,0:T(8,128)S(1)}, f32[5,768]{1,0:T(8,128)}, u32[]{:S(2)}) copy-start(f32[5,768]{1,0:T(8,128)} %copy-done.5) | copy-start | bytes 46084
  209.6 53.3 %all-to-all-start.3 = ((f32[4,192,640]{2,1,0:T(8,128)}), f32[4,192,640]{2,1,0:T(8,128)}, u32[]{:S(2)}, u32[]{:S(2)}) async-start(f32[4,192,640]{2,1,0:T(8,128)} %copy.43), calls=%async_computation.3 | async-start | bytes 3932160 | tf_op jit(solution)/shard_map/all_to_all | solution.py:84
  217.5 138.2 %reduce-scatter.4.cloned.1.call-start = ((), (), s32[]{:S(2)}) async-start(), calls=%async_computation.6 | async-start | bytes 2949120
Sparse Core Ops, SparseCore 0:
  272.6 83.1 reduce-scatter.3
